TPU v7x, 32 devices: a whole 2x2x4 slice. The times are simulated.
32 devices in a mesh: groups: 2 (over x), dp: 4 (over z), tensor: 4 (over y, core).
Axes of the slice: x: 2, y: 2, z: 4, core: 2. Of those that a mesh axis runs over, the one named last changes fastest.
Arguments:
- patches: float32 [16, 256, 6144], P(('groups', 'dp'), None, 'tensor'), parts along dimension 0, may hold values from -60 to 60
- counts: int32 [16], P(('groups', 'dp')), parts along dimension 0, may hold values from 1 to 63, as said below
- ranking: int32 [16, 256], P(('groups', 'dp')), parts along dimension 0, may hold values from 0 to 255, each once within a row
- norm_gain: float32 [6144], P('tensor'), may hold values from 0.1 to 1.9
- expand_weight: bfloat16 [24576, 6144], P(('dp', 'tensor')), may hold values from -0.078125 to 0.078125
- expand_bias: bfloat16 [24576], P(('dp', 'tensor')), may hold values from -4 to 4
- reduce_weight: bfloat16 [24576, 6144], P(('dp', 'tensor')), may hold values from -0.078125 to 0.078125
- reduce_bias: float32 [6144], P('tensor'), may hold values from -4 to 4
Outputs:
- updated: float32 [16, 256, 6144], P(('groups', 'dp'), None, 'tensor'), parts along dimension 0
There are 2 independent parts, one for each index of `groups`. A program takes and returns all parts, laid end to end along the dimension named above; an argument that names none is the same for every part. Nothing has to cross between parts.
Inputs may be any that keep to these rules, and one draw needn't show every extreme that they name: The counts of the 2 images of one index of dp (images b * 2 to (b + 1) * 2 - 1) sum to at most 64; in every draw one such group sums to exactly 64, and some image holds exactly 63.
All inputs are finite; a program needn't handle non-finite values.
Results may differ from a plain program's by a relative error of at most 0.00061.
Values may be sent and summed in bfloat16 or wider, within the bound.
A program may use at most 128 MiB of HBM per device.

v0:
```python
import jax
import jax.numpy as jnp
from jax import lax
from jax.sharding import PartitionSpec as P

D = 6144
CAP = 64


def body(
    patches, counts, ranking, norm_gain, expand_weight, expand_bias, reduce_weight, reduce_bias
):
    images, patch_len, width_local = patches.shape
    starts = jnp.cumsum(counts) - counts
    column = jnp.arange(CAP, dtype=jnp.int32)
    valid = column[None, :] < counts[:, None]
    target = jnp.where(valid, starts[:, None] + column[None, :], CAP).reshape(-1)
    source = (jnp.arange(images, dtype=jnp.int32)[:, None] * patch_len + ranking[:, :CAP]).reshape(
        -1
    )
    slot_source = jnp.zeros((CAP,), jnp.int32).at[target].set(source, mode="drop")
    slot_live = jnp.zeros((CAP,), jnp.float32).at[target].set(1.0, mode="drop")
    flat = patches.reshape(images * patch_len, width_local)
    rows = flat[slot_source]
    first, second = lax.psum((jnp.sum(rows, axis=1), jnp.sum(rows * rows, axis=1)), "tensor")
    mean = first[:, None] / D
    var = second[:, None] / D - mean * mean
    normed = ((rows - mean) * lax.rsqrt(var + 1e-06) * norm_gain).astype(jnp.bfloat16)
    full_rows = lax.all_gather(normed, "tensor", axis=1, tiled=True)
    pre = lax.dot_general(
        lax.all_gather(full_rows, "dp", axis=0, tiled=True),
        expand_weight,
        (((1,), (1,)), ((), ())),
        preferred_element_type=jnp.float32,
    )
    hidden = jax.nn.gelu(pre + expand_bias.astype(jnp.float32), approximate=True).astype(
        jnp.bfloat16
    )
    partial_value = jnp.dot(hidden, reduce_weight, preferred_element_type=jnp.float32)
    by_feature = lax.psum_scatter(partial_value, "tensor", scatter_dimension=1, tiled=True)
    branch = lax.psum_scatter(by_feature, "dp", scatter_dimension=0, tiled=True)
    update = slot_live[:, None] * (branch + reduce_bias)
    result = flat.at[slot_source].add(update)
    return result.reshape(images, patch_len, width_local)


def solution(mesh):
    placed = (
        P(("groups", "dp"), None, "tensor"),
        P(("groups", "dp")),
        P(("groups", "dp"), None),
        P("tensor"),
        P(("dp", "tensor"), None),
        P(("dp", "tensor")),
        P(("dp", "tensor"), None),
        P("tensor"),
    )
    return jax.shard_map(
        body,
        mesh=mesh,
        in_specs=placed,
        out_specs=P(("groups", "dp"), None, "tensor"),
        check_vma=False,
    )
```

profile of v0, /device:TPU:0, one launch (start us, length us, event | category | flops | bytes accessed | tf_op | source)
XLA Modules:
  0.0 220.5 jit_solution(17634967251671957816)
XLA Ops:
  6.5 0.0 copy-start.6
  6.5 0.0 copy-start.5
  6.5 0.0 all-gather.2.cloned.1.call-start
  6.5 1.9 copy.11
  8.5 0.0 copy-start.1
  8.5 0.0 copy-done.6
  8.5 0.2 reduce-window.9
  8.6 0.1 compare_select_fusion.2
  8.7 0.1 select_n.31
  8.8 0.0 copy-done.5
  8.8 0.0 copy-start.7
  8.8 0.1 slice_add_fusion
  8.9 0.1 reshape.126
  9.0 1.0 scatter_custom_fusion
  10.0 0.0 copy-start.4
  10.0 0.0 copy-done.7
  10.0 0.5 copy-done.4
  10.5 0.0 copy-start.3
  10.5 0.7 gather_fusion
  11.2 0.7 fusion.18
  11.9 9.0 %all-reduce = (f32[64]{0:T(128)}, f32[64]{0:T(128)}) all-reduce(f32[64]{0:T(128)} %get-tuple-element.6, f32[64]{0:T(128)S(1)} %get-tuple-element.5), channel_id=1, replica_groups=mesh['groups'=2,'dp'=4,'tensor'=4] {'tensor'}, use_global_device_ids=true, to_apply=%region_6.7 | all-reduce | flops 128 | bytes 1024 | tf_op jit(solution)/shard_map/psum | solution.py:25
  21.0 0.6 broadcast_multiply_fusion
  21.6 0.0 copy-done.1
  21.6 0.1 multiply_convert_fusion
  21.7 7.9 %all_gather.6 = bf16[64,6144]{1,0:T(8,128)(2,1)} all-gather(bf16[64,1536]{1,0:T(8,128)(2,1)S(1)} %multiply_convert_fusion), channel_id=1, replica_groups=mesh['groups'=2,'dp'=4,'tensor'=4] {'tensor'}, dimensions={1}, use_global_device_ids=true | all-gather | bytes 983040 | tf_op jit(solution)/shard_map/all_gather | solution.py:29
  29.6 0.0 all-gather.2.cloned.1.call-update
  29.7 0.0 reduce-scatter.3.cloned.1.call-start
  29.7 0.0 copy-done.3
  29.7 64.9 %all-gather.2.cloned.1.call-done = bf16[256,6144]{1,0:T(8,128)(2,1)} async-done(((bf16[64,6144]{1,0:T(8,128)(2,1)}), bf16[256,6144]{1,0:T(8,128)(2,1)}) %all-gather.2.cloned.1.call-update) | async-done | bytes 3145744 | tf_op jit(solution)/shard_map/all_gather | solution.py:31
  94.7 20.2 %fusion.19 = f32[256,6144]{1,0:T(8,128)} fusion(bf16[1536,6144]{1,0:T(8,128)(2,1)} %param.14, bf16[256,6144]{1,0:T(8,128)(2,1)} %all-gather.2.cloned.1.call-done, bf16[1536,6144]{1,0:T(8,128)(2,1)} %param.12, f32[1536]{0:T(1024)S(1)} %convert_element_type.10), kind=kOutput, calls=%fused_computation.36 | convolution fusion | flops 9667608576 | bytes 47192064 | tf_op jit(solution)/shard_map/dot_general | solution.py:39
  114.8 0.0 copy-start.2
  114.8 0.0 reduce-scatter.3.cloned.1.call-update
  114.9 0.0 reduce-scatter.5.cloned.1.call-start
  114.9 56.7 %reduce-scatter.3.cloned.1.call-done = f32[256,1536]{1,0:T(8,128)} async-done(((f32[256,6144]{1,0:T(8,128)}), f32[256,1536]{1,0:T(8,128)}) %reduce-scatter.3.cloned.1.call-update) | async-done | bytes 1572880 | tf_op jit(solution)/shard_map/reduce_scatter | solution.py:40
  171.6 0.0 reduce-scatter.5.cloned.1.call-update
  171.6 1.1 scatter_custom_fusion.1
  172.7 36.6 %reduce-scatter.5.cloned.1.call-done = f32[64,1536]{1,0:T(8,128)} async-done(((f32[256,1536]{1,0:T(8,128)}), f32[64,1536]{1,0:T(8,128)}) %reduce-scatter.5.cloned.1.call-update) | async-done | bytes 393232 | tf_op jit(solution)/shard_map/reduce_scatter | solution.py:41
  209.4 0.0 copy-done.2
  209.4 2.9 %scatter_custom_fusion.2 = f32[512,1536]{1,0:T(8,128)S(1)} fusion(f32[512,1536]{1,0:T(8,128)S(1)} %bitcast.22, s32[64]{0:T(128)} %copy-done.4, f32[64,1536]{1,0:T(8,128)} %reduce-scatter.5.cloned.1.call-done, f32[1536]{0:T(1024)S(1)} %copy-done.2, f32[64]{0:T(128)S(1)} %scatter_custom_fusion.1), kind=kCustom, calls=%fused_computation.14 | custom fusion | flops 294912 | bytes 3547648 | tf_op jit(solution)/shard_map/scatter-add | solution.py:43
  212.3 0.0 copy-start
  212.3 1.7 copy-done
  (7 shorter events, 0.0 us)
Async XLA Ops:
  6.5 1.9 copy-start.6
  6.5 2.3 %copy-start.5 = (s32[2,256]{1,0:T(2,128)S(1)}, s32[2,256]{1,0:T(2,128)}, u32[]{:S(2)}) copy-start(s32[2,256]{1,0:T(2,128)} %param.10) | copy-start | bytes 6148
  6.5 88.1 %all-gather.2.cloned.1.call-start = ((), (), s32[]{:S(2)}) async-start(), calls=%async_computation.2 | async-start | bytes 3932160 | tf_op jit(solution)/shard_map/all_gather | solution.py:31
  8.5 13.1 %copy-start.1 = (f32[1536]{0:T(1024)S(1)}, f32[1536]{0:T(1024)}, u32[]{:S(2)}) copy-start(f32[1536]{0:T(1024)} %param.11) | copy-start | bytes 18436
  8.8 1.2 copy-start.7
  10.0 0.5 copy-start.4
  10.5 19.2 %copy-start.3 = (bf16[1536]{0:T(1024)(128)(2,1)S(1)}, bf16[1536]{0:T(1024)(128)(2,1)}, u32[]{:S(2)}) copy-start(bf16[1536]{0:T(1024)(128)(2,1)} %param.13) | copy-start | bytes 9220
  29.7 141.9 %reduce-scatter.3.cloned.1.call-start = ((), (), s32[]{:S(2)}) async-start(), calls=%async_computation.3 | async-start | bytes 7864320 | tf_op jit(solution)/shard_map/reduce_scatter | solution.py:40
  114.8 94.5 %copy-start.2 = (f32[1536]{0:T(1024)S(1)}, f32[1536]{0:T(1024)}, u32[]{:S(2)}) copy-start(f32[1536]{0:T(1024)} %param.15) | copy-start | bytes 18436
  114.9 94.5 %reduce-scatter.5.cloned.1.call-start = ((), (), s32[]{:S(2)}) async-start(), calls=%async_computation.4 | async-start | bytes 1966080 | tf_op jit(solution)/shard_map/reduce_scatter | solution.py:41
  212.3 1.7 copy-start
Sparse Core Ops, SparseCore 0:
  29.8 64.8 all-gather.1
  115.0 56.5 reduce-scatter.2
  173.9 35.4 reduce-scatter.4
where the time goes:
time: 221 us; the launch traced here: 220 us
  waiting for transfers between devices  158 us (71%)
  matrix products  20.2 us (9%)
  blocking collectives  16.9 us (8%)
  between operations  13.2 us (6%)
  local copies, waits for them, and re-layouts  7.03 us (3%)
  other arithmetic  4.73 us (2%)
    all_gather x1, waiting for transfers between devices, body(): lax.all_gather(full_rows, 'dp', axis=0, tiled=True)  64.9 us
    reduce_scatter x1, waiting for transfers between devices, body(): lax.psum_scatter(partial_value, 'tensor', scatter_dimension=1, tiled=True)  56.7 us
    reduce_scatter x1, waiting for transfers between devices, body(): branch = lax.psum_scatter(by_feature, 'dp', scatter_dimension=0, tiled=True)  36.6 us
    dot_general x1, matrix products, body(): jnp.dot(hidden, reduce_weight, preferred_element_type=jnp.float32)  20.2 us
    psum x1, blocking collectives, body(): lax.psum((jnp.sum(rows, axis=1), jnp.sum(rows * rows, axis=1)), 'tensor')  9.03 us
    all_gather x1, blocking collectives, body(): full_rows = lax.all_gather(normed, 'tensor', axis=1, tiled=True)  7.92 us
  transfers between devices with their start and end apart: 3, of which 3 were waited for; matrix products, arithmetic and copies ran while one was open for 1% of the time, Pallas kernels for 0%

commit v1 on v0

v1 whole, which is shorter than its diff:
```python
import functools

import jax
import jax.numpy as jnp
from jax import lax
from jax.experimental import pallas as pl
from jax.experimental.pallas import tpu as pltpu
from jax.sharding import PartitionSpec as P

CAP = 64
MESH = pl.DeviceIdType.MESH


def gather_kernel(counts, ranking, flat, rows, sem):
    images, patch_len = ranking.shape

    def issue(j, carry):
        start, source = 0, 0
        for i in range(images):
            offset = j - start
            inside = (offset >= 0) & (offset < counts[i])
            place = ranking[i, jnp.clip(offset, 0, patch_len - 1)]
            source = jnp.where(inside, i * patch_len + place, source)
            start = start + counts[i]
        pltpu.make_async_copy(flat.at[pl.ds(source, 1)], rows.at[pl.ds(j, 1)], sem).start()
        return carry

    lax.fori_loop(0, CAP, issue, 0)
    pltpu.make_async_copy(rows, rows, sem).wait()


def update_kernel(counts, ranking, flat, update, out, buf, in_sem, out_sem):
    images, patch_len = ranking.shape

    def load(i):
        part = pl.ds(i * patch_len, patch_len)
        return pltpu.make_async_copy(flat.at[part], buf.at[part], in_sem.at[i])

    def save(i):
        part = pl.ds(i * patch_len, patch_len)
        return pltpu.make_async_copy(buf.at[part], out.at[part], out_sem.at[i])

    for i in range(images):
        load(i).start()
    start = 0
    for i in range(images):
        load(i).wait()

        def put(j, carry):
            buf[pl.ds(i * patch_len + ranking[i, j], 1), :] = update[pl.ds(carry + j, 1), :]
            return carry

        lax.fori_loop(0, counts[i], put, start)
        start = start + counts[i]
        save(i).start()
    for i in range(images):
        save(i).wait()


def block_kernel(
    Z, T, C, C2, rows, gain, ebias, rbias, e_hbm, r_hbm, out,
    xg, wv, rv, pre, hid, st, cs, cr, own, ys, yr, zs, zr,
    wsem, rsem, st_s, st_r, za_s, za_r, ya_s, ya_r, ca_s, ca_r,
    cr_s, cr_r, yr_s, yr_r, zr_s, zr_r,
):
    Y = T // 2
    R, dl = rows.shape
    hl, D = e_hbm.shape
    M, dlc, w2 = Z * R, dl // C, dl // C2
    nt = 256 if hl % 256 == 0 else hl
    z = lax.axis_index("dp")
    t = lax.axis_index("tensor")
    y, c = t // 2, t % 2
    z_next = lax.rem(z + 1, Z)
    t_next = lax.rem(y + 1, Y) * 2 + c
    t_part = y * 2 + 1 - c

    barrier = pltpu.get_barrier_semaphore()
    for k in range(1, Z):
        pl.semaphore_signal(barrier, inc=1, device_id={"dp": lax.rem(z + k, Z)}, device_id_type=MESH)
    for k in range(1, T):
        pl.semaphore_signal(barrier, inc=1, device_id={"tensor": lax.rem(t + k, T)}, device_id_type=MESH)

    def copy(src, dst, ss, rs, axis, index):
        return pltpu.make_async_remote_copy(
            src_ref=src, dst_ref=dst, send_sem=ss, recv_sem=rs,
            device_id={axis: index}, device_id_type=MESH,
        )

    def t_of(u, core):
        return lax.rem(y - u + Y, Y) * 2 + core

    def t_red(u, core):
        return lax.rem(y - 1 - u + 2 * Y, Y) * 2 + core

    order = []
    for u in range(Y):
        for core in (c, 1 - c):
            for p in range(C):
                order.append((t_of(u, core), p))

    def expand_load(i):
        block, p = order[i]
        lanes = pl.ds(pl.multiple_of(block * dl + p * dlc, 128), dlc)
        return pltpu.make_async_copy(e_hbm.at[:, lanes], wv.at[i], wsem.at[i])

    def reduce_load(i):
        block = t_red(i // 2, c if i % 2 == 0 else 1 - c)
        lanes = pl.ds(pl.multiple_of(block * dl, 128), dl)
        return pltpu.make_async_copy(r_hbm.at[:, lanes], rv.at[i], rsem.at[i])

    for i in range(T * C):
        expand_load(i).start()
    for i in range(T):
        reduce_load(i).start()

    x = rows[...]
    s1 = jnp.sum(x, axis=1, keepdims=True)
    s2 = jnp.sum(x * x, axis=1, keepdims=True)
    lane = lax.broadcasted_iota(jnp.int32, (R, 128), 1)
    st[t] = jnp.where(lane == 0, s1, s2)
    pl.semaphore_wait(barrier, Z + T - 2)

    def stat_copy(k):
        return copy(st.at[t], st.at[t], st_s.at[k - 1], st_r.at[k - 1], "tensor", lax.rem(t + k, T))

    for k in range(1, T):
        stat_copy(k).start()
    for k in range(1, T):
        stat_copy(k).wait_recv()
    total = st[0]
    for k in range(1, T):
        total = total + st[k]
    mean = total[:, 0:1] / D
    var = total[:, 1:2] / D - mean * mean
    scale = lax.rsqrt(var + 1e-06)
    mine = pl.ds(pl.multiple_of(z * R, R), R)
    for p in range(C):
        cols = slice(p * dlc, (p + 1) * dlc)
        xg[t, p, mine, :] = ((rows[:, cols] - mean) * scale * gain[:, cols]).astype(jnp.bfloat16)

    def block(tt, j, p):
        return xg.at[tt, p, pl.ds(pl.multiple_of(lax.rem(z - j + Z, Z) * R, R), R), :]

    def z_copy(s, p):
        b = block(t, s - 1, p)
        return copy(b, b, za_s.at[s - 1, p], za_r.at[s - 1, p], "dp", z_next)

    def y_copy(u, j, p):
        b = block(t_of(u - 1, c), j, p)
        return copy(b, b, ya_s.at[u - 1, j, p], ya_r.at[u - 1, j, p], "tensor", t_next)

    def c_copy(u, j, p):
        b = block(t_of(u, c), j, p)
        return copy(b, b, ca_s.at[u, j, p], ca_r.at[u, j, p], "tensor", t_part)

    def expand(i):
        tt, p = order[i]
        expand_load(i).wait()

        def tile(n):
            cols = slice(None) if nt == hl else pl.ds(pl.multiple_of(n * nt, nt), nt)
            acc = lax.dot_general(
                xg[tt, p], wv[i, cols, :], (((1,), (1,)), ((), ())),
                preferred_element_type=jnp.float32,
            )
            if i > 0:
                acc = acc + pre[:, cols]
            if i < T * C - 1:
                pre[:, cols] = acc
            else:
                v = acc + ebias[:, cols].astype(jnp.float32)
                hid[:, cols] = jax.nn.gelu(v, approximate=True).astype(jnp.bfloat16)

        if nt == hl:
            tile(0)
        else:
            lax.fori_loop(0, hl // nt, lambda n, a: (tile(n), a)[1], 0)

    def expand_partner(u, p):
        for j in range(Z):
            c_copy(u, j, p).wait_recv()
        expand((2 * u + 1) * C + p)

    def y_arrived(u, j, p):
        y_copy(u, j, p).wait_recv()
        if u < Y - 1:
            y_copy(u + 1, j, p).start()
        c_copy(u, j, p).start()

    for p in range(C):
        z_copy(1, p).start()
        y_copy(1, 0, p).start()
        c_copy(0, 0, p).start()
    for s in range(1, Z):
        for p in range(C):
            z_copy(s, p).wait_recv()
            if s < Z - 1:
                z_copy(s + 1, p).start()
            y_copy(1, s, p).start()
            c_copy(0, s, p).start()
            if s == Z - 1:
                expand(p)
        for p in range(C):
            y_arrived(1, s - 1, p)
    for p in range(C):
        expand_partner(0, p)
    for u in range(1, Y):
        for j in range(Z - 1 if u == 1 else 0, Z):
            for p in range(C):
                y_arrived(u, j, p)
                if j == Z - 1:
                    expand(2 * u * C + p)
        for p in range(C):
            expand_partner(u, p)

    def cr_copy(u, p):
        return copy(cs.at[u, p], cr.at[u, p], cr_s.at[u, p], cr_r.at[u, p], "tensor", t_part)

    def yr_copy(u, p):
        return copy(ys.at[u - 1, p], yr.at[u - 1, p], yr_s.at[u - 1, p], yr_r.at[u - 1, p], "tensor", t_next)

    def zr_copy(k, p):
        there = lax.rem(z + k, Z)
        part = pl.ds(pl.multiple_of(there * R, R), R)
        return copy(zs.at[p, part, :], zr.at[k - 1, p], zr_s.at[k - 1, p], zr_r.at[k - 1, p], "dp", there)

    def columns(p):
        return slice(None) if C2 == 1 else pl.ds(pl.multiple_of(p * w2, w2), w2)

    def product(i, p):
        return jnp.dot(hid[...], rv[i, :, columns(p)], preferred_element_type=jnp.float32)

    def produce(u, p):
        cs[u, p] = product(2 * u + 1, p).astype(jnp.bfloat16)
        cr_copy(u, p).start()
        own[u, p] = product(2 * u, p)

    def combine(u, p):
        cr_copy(u, p).wait_recv()
        v = own[u, p] + cr[u, p].astype(jnp.float32)
        if u == 0:
            ys[0, p] = v.astype(jnp.bfloat16)
            yr_copy(1, p).start()
        else:
            own[u, p] = v

    def loop(low, high, body):
        lax.fori_loop(low, high, lambda p, a: (body(p), a)[1], 0)

    for u in range(Y):
        reduce_load(2 * u).wait()
        reduce_load(2 * u + 1).wait()
        produce(u, 0)
        if u > 0:
            combine(u - 1, C2 - 1)

        def step(p):
            produce(u, p)
            combine(u, p - 1)

        if C2 > 1:
            loop(1, C2, step)
    combine(Y - 1, C2 - 1)

    for u in range(1, Y):

        def pass_on(p):
            yr_copy(u, p).wait_recv()
            v = own[u, p] + yr[u - 1, p].astype(jnp.float32)
            if u < Y - 1:
                ys[u, p] = v.astype(jnp.bfloat16)
                yr_copy(u + 1, p).start()
            else:
                own[u, p] = v
                zs[p] = v.astype(jnp.bfloat16)
                for k in range(1, Z):
                    zr_copy(k, p).start()

        loop(0, C2, pass_on)

    def finish(p):
        acc = own[Y - 1, p, mine, :]
        for k in range(1, Z):
            zr_copy(k, p).wait_recv()
            acc = acc + zr[k - 1, p].astype(jnp.float32)
        cols = columns(p)
        out[:, cols] = rows[:, cols] + (acc + rbias[:, cols])

    loop(0, C2, finish)

    for k in range(1, T):
        stat_copy(k).wait_send()
    for p in range(C):
        for s in range(1, Z):
            z_copy(s, p).wait_send()
        for j in range(Z):
            for u in range(1, Y):
                y_copy(u, j, p).wait_send()
            for u in range(Y):
                c_copy(u, j, p).wait_send()

    def drain(p):
        for u in range(Y):
            cr_copy(u, p).wait_send()
        for u in range(1, Y):
            yr_copy(u, p).wait_send()
        for k in range(1, Z):
            zr_copy(k, p).wait_send()

    loop(0, C2, drain)


def body(
    Z, T, patches, counts, ranking, norm_gain, expand_weight, expand_bias, reduce_weight, reduce_bias
):
    images, patch_len, dl = patches.shape
    hl, D = expand_weight.shape
    flat = patches.reshape(images * patch_len, dl)
    R, M, Y = CAP, Z * CAP, T // 2
    C = 3 if dl % 768 == 0 else 1
    w2 = 256 if dl % 256 == 0 else dl
    C2 = dl // w2
    dlc = dl // C
    vmem = pl.BlockSpec(memory_space=pltpu.VMEM)
    hbm = pl.BlockSpec(memory_space=pl.ANY)
    bf16, f32 = jnp.bfloat16, jnp.float32
    rows = pl.pallas_call(
        gather_kernel,
        out_shape=jax.ShapeDtypeStruct((R, dl), f32),
        grid_spec=pltpu.PrefetchScalarGridSpec(
            num_scalar_prefetch=2, grid=(), in_specs=[hbm], out_specs=vmem,
            scratch_shapes=[pltpu.SemaphoreType.DMA],
        ),
        name="gather_rows",
    )(counts, ranking, flat)
    dma = pltpu.SemaphoreType.DMA
    update = pl.pallas_call(
        functools.partial(block_kernel, Z, T, C, C2),
        out_shape=jax.ShapeDtypeStruct((R, dl), f32),
        in_specs=[vmem] * 4 + [hbm] * 2,
        out_specs=vmem,
        scratch_shapes=[
            pltpu.VMEM((T, C, M, dlc), bf16),
            pltpu.VMEM((T * C, hl, dlc), bf16),
            pltpu.VMEM((T, hl, dl), bf16),
            pltpu.VMEM((M, hl), f32),
            pltpu.VMEM((M, hl), bf16),
            pltpu.VMEM((T, R, 128), f32),
            pltpu.VMEM((Y, C2, M, w2), bf16),
            pltpu.VMEM((Y, C2, M, w2), bf16),
            pltpu.VMEM((Y, C2, M, w2), f32),
            pltpu.VMEM((Y - 1, C2, M, w2), bf16),
            pltpu.VMEM((Y - 1, C2, M, w2), bf16),
            pltpu.VMEM((C2, M, w2), bf16),
            pltpu.VMEM((Z - 1, C2, R, w2), bf16),
            dma((T * C,)), dma((T,)),
            dma((T - 1,)), dma((T - 1,)),
            dma((Z - 1, C)), dma((Z - 1, C)),
            dma((Y - 1, Z, C)), dma((Y - 1, Z, C)),
            dma((Y, Z, C)), dma((Y, Z, C)),
            dma((Y, C2)), dma((Y, C2)),
            dma((Y - 1, C2)), dma((Y - 1, C2)),
            dma((Z - 1, C2)), dma((Z - 1, C2)),
        ],
        compiler_params=pltpu.CompilerParams(
            collective_id=0, has_side_effects=True, vmem_limit_bytes=67000000
        ),
        name="feed_forward",
    )(
        rows, norm_gain.reshape(1, dl), expand_bias.reshape(1, hl), reduce_bias.reshape(1, dl),
        expand_weight, reduce_weight,
    )
    result = pl.pallas_call(
        update_kernel,
        out_shape=jax.ShapeDtypeStruct((images * patch_len, dl), f32),
        grid_spec=pltpu.PrefetchScalarGridSpec(
            num_scalar_prefetch=2, grid=(), in_specs=[hbm, vmem], out_specs=hbm,
            scratch_shapes=[
                pltpu.VMEM((images * patch_len, dl), f32),
                dma((images,)), dma((images,)),
            ],
        ),
        name="update_rows",
    )(counts, ranking, flat, update)
    return result.reshape(images, patch_len, dl)


def solution(mesh):
    placed = (
        P(("groups", "dp"), None, "tensor"),
        P(("groups", "dp")),
        P(("groups", "dp"), None),
        P("tensor"),
        P(("dp", "tensor"), None),
        P(("dp", "tensor")),
        P(("dp", "tensor"), None),
        P("tensor"),
    )
    return jax.shard_map(
        functools.partial(body, mesh.shape["dp"], mesh.shape["tensor"]),
        mesh=mesh,
        in_specs=placed,
        out_specs=P(("groups", "dp"), None, "tensor"),
        check_vma=False,
    )
```

time: 221 us -> 90 us (0.41)
  waiting for transfers between devices: 158 us -> 0 us
  Pallas kernels: 0 us -> 85.9 us
  matrix products: 20.2 us -> 0 us
  blocking collectives: 16.9 us -> 0 us
  between operations: 13.2 us -> 0.02 us
  other arithmetic: 4.73 us -> 0 us
  local copies, waits for them, and re-layouts: 7.03 us -> 3.86 us
    reduce_scatter x2 -> x0, waiting for transfers between devices: 93.3 us -> none  [the longest x1 56.7 us: body(): lax.psum_scatter(partial_value, 'tensor', scatter_dimension=1, tiled=True)]
    pallas_call x0 -> x3, Pallas kernels: none -> 85.9 us  [the longest x1 77.2 us: body(): pl.pallas_call(functools.partial(block_kernel, Z, T, C, C2), out_shape=ja...]
    all_gather x1 -> x0, waiting for transfers between devices: 64.9 us -> none  [body(): lax.all_gather(full_rows, 'dp', axis=0, tiled=True)]
    dot_general x1 -> x0, matrix products: 20.2 us -> none  [body(): jnp.dot(hidden, reduce_weight, preferred_element_type=jnp.float32)]
    psum x1 -> x0, blocking collectives: 9.03 us -> none  [body(): lax.psum((jnp.sum(rows, axis=1), jnp.sum(rows * rows, axis=1)), 'tensor')]
    all_gather x1 -> x0, blocking collectives: 7.92 us -> none  [body(): full_rows = lax.all_gather(normed, 'tensor', axis=1, tiled=True)]
    unnamed x17 -> x0, local copies, waits for them, and re-layouts: 4.08 us -> none
    reshape x1 -> x3, local copies, waits for them, and re-layouts: 0.08 us -> 3.86 us  [the longest x1 1.3 us: body(): reduce_bias.reshape(1, dl)]
  transfers between devices with their start and end apart: 3 -> 0, of which waited for: 3 -> 0; matrix products, arithmetic and copies ran while one was open for 1% -> 0% of each run, Pallas kernels for 0% -> 0%
where the time goes in v1:
time: 90 us; the launch traced here: 89.8 us
  Pallas kernels  85.9 us (95%)
  local copies, waits for them, and re-layouts  3.86 us (4%)
    pallas_call x1, Pallas kernels, body(): pl.pallas_call(functools.partial(block_kernel, Z, T, C, C2), out_shape=ja...  77.2 us
    pallas_call x1, Pallas kernels, body(): pl.pallas_call(update_kernel, out_shape=jax.ShapeDtypeStruct((images * pa...  5.17 us
    pallas_call x1, Pallas kernels, body(): pl.pallas_call(gather_kernel, out_shape=jax.ShapeDtypeStruct((R, dl), f32...  3.51 us

profile of v1, /device:TPU:0, one launch (start us, length us, event | category | flops | bytes accessed | tf_op | source)
XLA Modules:
  0.0 89.8 jit_solution(17968925472466193277)
XLA Ops:
  0.0 1.3 %reshape.16.gain = f32[1,1536]{1,0:T(1,128)} reshape(f32[1536]{0:T(1024)} %param.11) | data formatting | bytes 12288 | tf_op jit(solution)/shard_map/reshape | solution.py:371
  1.3 1.3 %reshape.17.ebias = bf16[1,1536]{1,0:T(2,128)(2,1)} reshape(bf16[1536]{0:T(1024)(128)(2,1)} %param.13) | data formatting | bytes 6144 | tf_op jit(solution)/shard_map/reshape | solution.py:371
  2.6 1.3 %reshape.18.rbias = f32[1,1536]{1,0:T(1,128)} reshape(f32[1536]{0:T(1024)} %param.15) | data formatting | bytes 12288 | tf_op jit(solution)/shard_map/reshape | solution.py:371
  3.9 3.5 %gather_rows.1.rows = f32[64,1536]{1,0:T(8,128)} custom-call(s32[2]{0:T(128)} %counts.3, s32[2,256]{1,0:T(2,128)} %ranking.3, f32[512,1536]{1,0:T(8,128)} %bitcast.2), custom_call_target="tpu_custom_call" | custom-call | tf_op jit(solution)/shard_map/gather_rows/pallas_call | solution.py:328
  7.4 77.2 %feed_forward.1.update = f32[64,1536]{1,0:T(8,128)} custom-call(f32[64,1536]{1,0:T(8,128)} %gather_rows.1.rows, f32[1,1536]{1,0:T(1,128)} %reshape.16.gain, bf16[1,1536]{1,0:T(2,128)(2,1)} %reshape.17.ebias, f32[1,1536]{1,0:T(1,128)} %reshape.18.rbias, bf16[1536,6144]{1,0:T(8,128)(2,1)} %e_hbm.1, bf16[1536,6144]{1,0:T(8,128)(2,1)} %r_hbm.1), custom_call_target="tpu_custom_call" | custom-call | tf_op jit(solution)/shard_map/feed_forward/pallas_call | solution.py:338
  84.6 5.2 %update_rows.1 = f32[512,1536]{1,0:T(8,128)} custom-call(s32[2]{0:T(128)} %counts.3, s32[2,256]{1,0:T(2,128)} %ranking.3, f32[512,1536]{1,0:T(8,128)} %bitcast.3, f32[64,1536]{1,0:T(8,128)} %feed_forward.1.update), custom_call_target="tpu_custom_call" | custom-call | tf_op jit(solution)/shard_map/update_rows/pallas_call | solution.py:374

commit v2 on v1

--- a/solution.py
+++ b/solution.py
@@ -11,60 +11,16 @@
 MESH = pl.DeviceIdType.MESH
 
 
-def gather_kernel(counts, ranking, flat, rows, sem):
-    images, patch_len = ranking.shape
-
-    def issue(j, carry):
-        start, source = 0, 0
-        for i in range(images):
-            offset = j - start
-            inside = (offset >= 0) & (offset < counts[i])
-            place = ranking[i, jnp.clip(offset, 0, patch_len - 1)]
-            source = jnp.where(inside, i * patch_len + place, source)
-            start = start + counts[i]
-        pltpu.make_async_copy(flat.at[pl.ds(source, 1)], rows.at[pl.ds(j, 1)], sem).start()
-        return carry
-
-    lax.fori_loop(0, CAP, issue, 0)
-    pltpu.make_async_copy(rows, rows, sem).wait()
-
-
-def update_kernel(counts, ranking, flat, update, out, buf, in_sem, out_sem):
-    images, patch_len = ranking.shape
-
-    def load(i):
-        part = pl.ds(i * patch_len, patch_len)
-        return pltpu.make_async_copy(flat.at[part], buf.at[part], in_sem.at[i])
-
-    def save(i):
-        part = pl.ds(i * patch_len, patch_len)
-        return pltpu.make_async_copy(buf.at[part], out.at[part], out_sem.at[i])
-
-    for i in range(images):
-        load(i).start()
-    start = 0
-    for i in range(images):
-        load(i).wait()
-
-        def put(j, carry):
-            buf[pl.ds(i * patch_len + ranking[i, j], 1), :] = update[pl.ds(carry + j, 1), :]
-            return carry
-
-        lax.fori_loop(0, counts[i], put, start)
-        start = start + counts[i]
-        save(i).start()
-    for i in range(images):
-        save(i).wait()
-
-
 def block_kernel(
-    Z, T, C, C2, rows, gain, ebias, rbias, e_hbm, r_hbm, out,
-    xg, wv, rv, pre, hid, st, cs, cr, own, ys, yr, zs, zr,
-    wsem, rsem, st_s, st_r, za_s, za_r, ya_s, ya_r, ca_s, ca_r,
+    Z, T, C, C2, counts, ranking, ranking_v, gain, ebias, rbias, flat, e_hbm, r_hbm, out,
+    pt, rows, pick,    xg, wv, rv, pre, hid, bias, last, st, cs, cr, own, ys, yr, zs, zr,
+    psem, osem, wsem, rsem, st_s, st_r, za_s, za_r, ya_s, ya_r, ca_s, ca_r,
     cr_s, cr_r, yr_s, yr_r, zr_s, zr_r,
 ):
     Y = T // 2
     R, dl = rows.shape
+    images, patch_len = ranking.shape
+    N = images * patch_len
     hl, D = e_hbm.shape
     M, dlc, w2 = Z * R, dl // C, dl // C2
     nt = 256 if hl % 256 == 0 else hl
@@ -109,11 +65,46 @@
         lanes = pl.ds(pl.multiple_of(block * dl, 128), dl)
         return pltpu.make_async_copy(r_hbm.at[:, lanes], rv.at[i], rsem.at[i])
 
+    patch_load = pltpu.make_async_copy(flat, pt, psem)
+    patch_load.start()
+
+    lane_w = images * R
+    which = lax.broadcasted_iota(jnp.int32, (1, lane_w), 1)
+    rank, owner = jnp.full((1, lane_w), -1, jnp.int32), jnp.full((1, lane_w), -1, jnp.int32)
+    start = 0
+    for i in range(images):
+        k = which - i * R
+        live = (k >= 0) & (k < counts[i])
+        owner = jnp.where(live, start + k, owner)
+        start = start + counts[i]
+        known = jnp.concatenate([ranking_v[i : i + 1, :R]] * images, axis=1)
+        rank = jnp.where(live, i * patch_len + known, rank)
+    chosen = jnp.where(lax.broadcasted_iota(jnp.int32, (N, lane_w), 0) == rank, 1.0, 0.0)
+    slot = jnp.where(lax.broadcasted_iota(jnp.int32, (R, lane_w), 0) == owner, 1.0, 0.0)
+    pick[...] = lax.dot_general(
+        chosen.astype(jnp.bfloat16), slot.astype(jnp.bfloat16), (((1,), (1,)), ((), ())),
+        preferred_element_type=jnp.float32,
+    ).astype(jnp.bfloat16)
+
+    def take(j, carry):
+        start, source = 0, 0
+        for i in range(images):
+            offset = j - start
+            inside = (offset >= 0) & (offset < counts[i])
+            here = i * patch_len + ranking[i, jnp.clip(offset, 0, patch_len - 1)]
+            source = jnp.where(inside, here, source)
+            start = start + counts[i]
+        rows[pl.ds(j, 1), :] = pt[pl.ds(source, 1), :]
+        return carry
+
+    patch_load.wait()
     for i in range(T * C):
         expand_load(i).start()
     for i in range(T):
         reduce_load(i).start()
-
+    lax.fori_loop(0, R, take, 0, unroll=8)
+
+    bias[...] = ebias[...].astype(jnp.float32)[None, :]
     x = rows[...]
     s1 = jnp.sum(x, axis=1, keepdims=True)
     s2 = jnp.sum(x * x, axis=1, keepdims=True)
@@ -131,13 +122,14 @@
     total = st[0]
     for k in range(1, T):
         total = total + st[k]
+    gain_row = gain[...][None, :]
     mean = total[:, 0:1] / D
     var = total[:, 1:2] / D - mean * mean
     scale = lax.rsqrt(var + 1e-06)
     mine = pl.ds(pl.multiple_of(z * R, R), R)
     for p in range(C):
         cols = slice(p * dlc, (p + 1) * dlc)
-        xg[t, p, mine, :] = ((rows[:, cols] - mean) * scale * gain[:, cols]).astype(jnp.bfloat16)
+        xg[t, p, mine, :] = ((rows[:, cols] - mean) * scale * gain_row[:, cols]).astype(jnp.bfloat16)
 
     def block(tt, j, p):
         return xg.at[tt, p, pl.ds(pl.multiple_of(lax.rem(z - j + Z, Z) * R, R), R), :]
@@ -158,24 +150,10 @@
         tt, p = order[i]
         expand_load(i).wait()
 
-        def tile(n):
-            cols = slice(None) if nt == hl else pl.ds(pl.multiple_of(n * nt, nt), nt)
-            acc = lax.dot_general(
-                xg[tt, p], wv[i, cols, :], (((1,), (1,)), ((), ())),
-                preferred_element_type=jnp.float32,
-            )
-            if i > 0:
-                acc = acc + pre[:, cols]
-            if i < T * C - 1:
-                pre[:, cols] = acc
-            else:
-                v = acc + ebias[:, cols].astype(jnp.float32)
-                hid[:, cols] = jax.nn.gelu(v, approximate=True).astype(jnp.bfloat16)
-
-        if nt == hl:
-            tile(0)
-        else:
-            lax.fori_loop(0, hl // nt, lambda n, a: (tile(n), a)[1], 0)
+        acc = lax.dot_general(
+            wv[i], xg[tt, p], (((1,), (1,)), ((), ())), preferred_element_type=jnp.float32
+        )
+        pre[...] = acc if i == 0 else pre[...] + acc
 
     def expand_partner(u, p):
         for j in range(Z):
@@ -214,6 +192,16 @@
         for p in range(C):
             expand_partner(u, p)
 
+    def activate(n):
+        units = slice(None) if nt == hl else pl.ds(pl.multiple_of(n * nt, nt), nt)
+        v = pre[units, :].T + bias[:, units]
+        hid[:, units] = jax.nn.gelu(v, approximate=True).astype(jnp.bfloat16)
+
+    if nt == hl:
+        activate(0)
+    else:
+        lax.fori_loop(0, hl // nt, lambda n, a: (activate(n), a)[1], 0)
+
     def cr_copy(u, p):
         return copy(cs.at[u, p], cr.at[u, p], cr_s.at[u, p], cr_r.at[u, p], "tensor", t_part)
 
@@ -279,13 +267,28 @@
 
         loop(0, C2, pass_on)
 
+    last[...] = rbias[...][None, :]
+
     def finish(p):
         acc = own[Y - 1, p, mine, :]
         for k in range(1, Z):
             zr_copy(k, p).wait_recv()
             acc = acc + zr[k - 1, p].astype(jnp.float32)
         cols = columns(p)
-        out[:, cols] = rows[:, cols] + (acc + rbias[:, cols])
+        add = acc + last[:, cols]
+        top = add.astype(jnp.bfloat16)
+        rest = add - top.astype(jnp.float32)
+        middle = rest.astype(jnp.bfloat16)
+        low = (rest - middle.astype(jnp.float32)).astype(jnp.bfloat16)
+        spread = jnp.dot(pick[...], low, preferred_element_type=jnp.float32)
+        spread = spread + jnp.dot(pick[...], middle, preferred_element_type=jnp.float32)
+        spread = spread + jnp.dot(pick[...], top, preferred_element_type=jnp.float32)
+        pt[:, cols] = pt[:, cols] + spread
+        save(p).start()
+
+    def save(p):
+        cols = columns(p)
+        return pltpu.make_async_copy(pt.at[:, cols], out.at[:, cols], osem.at[p])
 
     loop(0, C2, finish)
 
@@ -301,6 +304,7 @@
                 c_copy(u, j, p).wait_send()
 
     def drain(p):
+        save(p).wait()
         for u in range(Y):
             cr_copy(u, p).wait_send()
         for u in range(1, Y):
@@ -319,33 +323,31 @@
     flat = patches.reshape(images * patch_len, dl)
     R, M, Y = CAP, Z * CAP, T // 2
     C = 3 if dl % 768 == 0 else 1
-    w2 = 256 if dl % 256 == 0 else dl
+    w2 = 384 if dl % 384 == 0 else dl
     C2 = dl // w2
     dlc = dl // C
     vmem = pl.BlockSpec(memory_space=pltpu.VMEM)
     hbm = pl.BlockSpec(memory_space=pl.ANY)
     bf16, f32 = jnp.bfloat16, jnp.float32
-    rows = pl.pallas_call(
-        gather_kernel,
-        out_shape=jax.ShapeDtypeStruct((R, dl), f32),
-        grid_spec=pltpu.PrefetchScalarGridSpec(
-            num_scalar_prefetch=2, grid=(), in_specs=[hbm], out_specs=vmem,
-            scratch_shapes=[pltpu.SemaphoreType.DMA],
-        ),
-        name="gather_rows",
-    )(counts, ranking, flat)
     dma = pltpu.SemaphoreType.DMA
-    update = pl.pallas_call(
+    N = images * patch_len
+    smem = pl.BlockSpec(memory_space=pltpu.SMEM)
+    result = pl.pallas_call(
         functools.partial(block_kernel, Z, T, C, C2),
-        out_shape=jax.ShapeDtypeStruct((R, dl), f32),
-        in_specs=[vmem] * 4 + [hbm] * 2,
-        out_specs=vmem,
+        out_shape=jax.ShapeDtypeStruct((N, dl), f32),
+        in_specs=[smem] * 2 + [vmem] * 4 + [hbm] * 3,
+        out_specs=hbm,
         scratch_shapes=[
+            pltpu.VMEM((N, dl), f32),
+            pltpu.VMEM((R, dl), f32),
+            pltpu.VMEM((N, R), bf16),
             pltpu.VMEM((T, C, M, dlc), bf16),
             pltpu.VMEM((T * C, hl, dlc), bf16),
             pltpu.VMEM((T, hl, dl), bf16),
-            pltpu.VMEM((M, hl), f32),
+            pltpu.VMEM((hl, M), f32),
             pltpu.VMEM((M, hl), bf16),
+            pltpu.VMEM((1, hl), f32),
+            pltpu.VMEM((1, dl), f32),
             pltpu.VMEM((T, R, 128), f32),
             pltpu.VMEM((Y, C2, M, w2), bf16),
             pltpu.VMEM((Y, C2, M, w2), bf16),
@@ -354,7 +356,7 @@
             pltpu.VMEM((Y - 1, C2, M, w2), bf16),
             pltpu.VMEM((C2, M, w2), bf16),
             pltpu.VMEM((Z - 1, C2, R, w2), bf16),
-            dma((T * C,)), dma((T,)),
+            dma, dma((C2,)), dma((T * C,)), dma((T,)),
             dma((T - 1,)), dma((T - 1,)),
             dma((Z - 1, C)), dma((Z - 1, C)),
             dma((Y - 1, Z, C)), dma((Y - 1, Z, C)),
@@ -368,21 +370,8 @@
         ),
         name="feed_forward",
     )(
-        rows, norm_gain.reshape(1, dl), expand_bias.reshape(1, hl), reduce_bias.reshape(1, dl),
-        expand_weight, reduce_weight,
+        counts, ranking, ranking, norm_gain, expand_bias, reduce_bias, flat, expand_weight, reduce_weight,
     )
-    result = pl.pallas_call(
-        update_kernel,
-        out_shape=jax.ShapeDtypeStruct((images * patch_len, dl), f32),
-        grid_spec=pltpu.PrefetchScalarGridSpec(
-            num_scalar_prefetch=2, grid=(), in_specs=[hbm, vmem], out_specs=hbm,
-            scratch_shapes=[
-                pltpu.VMEM((images * patch_len, dl), f32),
-                dma((images,)), dma((images,)),
-            ],
-        ),
-        name="update_rows",
-    )(counts, ranking, flat, update)
     return result.reshape(images, patch_len, dl)
 
 

time: 90 us -> 71 us (0.79)
  Pallas kernels: 85.9 us -> 67.1 us
    pallas_call x1, Pallas kernels: 77.2 us -> 67.1 us  [body(): pl.pallas_call(functools.partial(block_kernel, Z, T, C, C2), out_shape=ja...]
    pallas_call x2 -> x0, Pallas kernels: 8.68 us -> none  [the longest x1 5.17 us: body(): pl.pallas_call(update_kernel, out_shape=jax.ShapeDtypeStruct((images * pa...]
    reshape x3 -> x0, local copies, waits for them, and re-layouts: 3.86 us -> none  [the longest x1 1.3 us: body(): reduce_bias.reshape(1, dl)]
    unnamed x0 -> x1, local copies, waits for them, and re-layouts: none -> 3.76 us
where the time goes in v2:
time: 71 us; the launch traced here: 70.8 us
  Pallas kernels  67.1 us (95%)
  local copies, waits for them, and re-layouts  3.76 us (5%)
    pallas_call x1, Pallas kernels, body(): pl.pallas_call(functools.partial(block_kernel, Z, T, C, C2), out_shape=ja...  67.1 us
    unnamed x1, local copies, waits for them, and re-layouts  3.76 us

profile of v2, /device:TPU:0, one launch (start us, length us, event | category | flops | bytes accessed | tf_op | source)
XLA Modules:
  0.0 70.8 jit_solution(7138041028684213233)
XLA Ops:
  0.0 67.1 %feed_forward.1 = f32[512,1536]{1,0:T(8,128)} custom-call(s32[2]{0:T(128)} %counts.1, s32[2,256]{1,0:T(2,128)} %ranking_v.1, s32[2,256]{1,0:T(2,128)} %ranking_v.1, f32[1536]{0:T(1024)} %gain.1, bf16[1536]{0:T(1024)(128)(2,1)} %ebias.1, f32[1536]{0:T(1024)} %rbias.1, f32[512,1536]{1,0:T(8,128)} %bitcast.3, bf16[1536,6144]{1,0:T(8,128)(2,1)} %e_hbm.1, ...), custom_call_target="tpu_custom_call" | custom-call | tf_op jit(solution)/shard_map/feed_forward/pallas_call | solution.py:335
  67.1 3.8 %copy.10 = f32[2,256,1536]{2,1,0:T(8,128)} copy(f32[2,256,1536]{2,1,0:T(8,128)} %bitcast.2) | data formatting | bytes 6291456

commit v3 on v2

--- a/solution.py
+++ b/solution.py
@@ -189,8 +189,9 @@
                 y_arrived(u, j, p)
                 if j == Z - 1:
                     expand(2 * u * C + p)
-        for p in range(C):
-            expand_partner(u, p)
+                    if p > 0:
+                        expand_partner(u, p - 1)
+        expand_partner(u, C - 1)
 
     def activate(n):
         units = slice(None) if nt == hl else pl.ds(pl.multiple_of(n * nt, nt), nt)
@@ -205,8 +206,12 @@
     def cr_copy(u, p):
         return copy(cs.at[u, p], cr.at[u, p], cr_s.at[u, p], cr_r.at[u, p], "tensor", t_part)
 
-    def yr_copy(u, p):
-        return copy(ys.at[u - 1, p], yr.at[u - 1, p], yr_s.at[u - 1, p], yr_r.at[u - 1, p], "tensor", t_next)
+    def yr_copy(u, p, h):
+        half = slice(h * M // 2, (h + 1) * M // 2)
+        return copy(
+            ys.at[u - 1, p, half, :], yr.at[u - 1, p, half, :],
+            yr_s.at[u - 1, p, h], yr_r.at[u - 1, p, h], "tensor", t_next,
+        )
 
     def zr_copy(k, p):
         there = lax.rem(z + k, Z)
@@ -229,7 +234,8 @@
         v = own[u, p] + cr[u, p].astype(jnp.float32)
         if u == 0:
             ys[0, p] = v.astype(jnp.bfloat16)
-            yr_copy(1, p).start()
+            for h in range(2):
+                yr_copy(1, p, h).start()
         else:
             own[u, p] = v
 
@@ -254,16 +260,21 @@
     for u in range(1, Y):
 
         def pass_on(p):
-            yr_copy(u, p).wait_recv()
-            v = own[u, p] + yr[u - 1, p].astype(jnp.float32)
-            if u < Y - 1:
-                ys[u, p] = v.astype(jnp.bfloat16)
-                yr_copy(u + 1, p).start()
-            else:
-                own[u, p] = v
-                zs[p] = v.astype(jnp.bfloat16)
-                for k in range(1, Z):
-                    zr_copy(k, p).start()
+            for h in range(2):
+                yr_copy(u, p, h).wait_recv()
+                half = slice(h * M // 2, (h + 1) * M // 2)
+                v = own[u, p, half, :] + yr[u - 1, p, half, :].astype(jnp.float32)
+                if u < Y - 1:
+                    ys[u, p, half, :] = v.astype(jnp.bfloat16)
+                    yr_copy(u + 1, p, h).start()
+                else:
+                    own[u, p, half, :] = v
+                    zs[p, half, :] = v.astype(jnp.bfloat16)
+                    for there in range(h * Z // 2, (h + 1) * Z // 2):
+
+                        @pl.when(there != z)
+                        def _():
+                            zr_copy(lax.rem(there - z + Z, Z), p).start()
 
         loop(0, C2, pass_on)
 
@@ -308,7 +319,8 @@
         for u in range(Y):
             cr_copy(u, p).wait_send()
         for u in range(1, Y):
-            yr_copy(u, p).wait_send()
+            for h in range(2):
+                yr_copy(u, p, h).wait_send()
         for k in range(1, Z):
             zr_copy(k, p).wait_send()
 
@@ -323,7 +335,7 @@
     flat = patches.reshape(images * patch_len, dl)
     R, M, Y = CAP, Z * CAP, T // 2
     C = 3 if dl % 768 == 0 else 1
-    w2 = 384 if dl % 384 == 0 else dl
+    w2 = 512 if dl % 512 == 0 else dl
     C2 = dl // w2
     dlc = dl // C
     vmem = pl.BlockSpec(memory_space=pltpu.VMEM)
@@ -362,7 +374,7 @@
             dma((Y - 1, Z, C)), dma((Y - 1, Z, C)),
             dma((Y, Z, C)), dma((Y, Z, C)),
             dma((Y, C2)), dma((Y, C2)),
-            dma((Y - 1, C2)), dma((Y - 1, C2)),
+            dma((Y - 1, C2, 2)), dma((Y - 1, C2, 2)),
             dma((Z - 1, C2)), dma((Z - 1, C2)),
         ],
         compiler_params=pltpu.CompilerParams(

time: 71 us -> 68.6 us (0.966)
  Pallas kernels: 67.1 us -> 64.6 us
    pallas_call x1, Pallas kernels: 67.1 us -> 64.6 us  [body(): pl.pallas_call(functools.partial(block_kernel, Z, T, C, C2), out_shape=ja...]
where the time goes in v3:
time: 68.6 us; the launch traced here: 68.4 us
  Pallas kernels  64.6 us (94%)
  local copies, waits for them, and re-layouts  3.76 us (5%)
    pallas_call x1, Pallas kernels, body(): pl.pallas_call(functools.partial(block_kernel, Z, T, C, C2), out_shape=ja...  64.6 us
    unnamed x1, local copies, waits for them, and re-layouts  3.76 us

profile of v3, /device:TPU:0, one launch (start us, length us, event | category | flops | bytes accessed | tf_op | source)
XLA Modules:
  0.0 68.4 jit_solution(13421576317221783362)
XLA Ops:
  0.0 64.6 %feed_forward.1 = f32[512,1536]{1,0:T(8,128)} custom-call(s32[2]{0:T(128)} %counts.1, s32[2,256]{1,0:T(2,128)} %ranking_v.1, s32[2,256]{1,0:T(2,128)} %ranking_v.1, f32[1536]{0:T(1024)} %gain.1, bf16[1536]{0:T(1024)(128)(2,1)} %ebias.1, f32[1536]{0:T(1024)} %rbias.1, f32[512,1536]{1,0:T(8,128)} %bitcast.3, bf16[1536,6144]{1,0:T(8,128)(2,1)} %e_hbm.1, ...), custom_call_target="tpu_custom_call" | custom-call | tf_op jit(solution)/shard_map/feed_forward/pallas_call | solution.py:347
  64.6 3.8 %copy.10 = f32[2,256,1536]{2,1,0:T(8,128)} copy(f32[2,256,1536]{2,1,0:T(8,128)} %bitcast.2) | data formatting | bytes 6291456
